TPU v7x, 32 devices: a whole 2x2x4 slice. The times are simulated.
32 devices in a mesh: groups: 2 (over x), row: 16 (over z, y, core).
Axes of the slice: x: 2, y: 2, z: 4, core: 2. Of those that a mesh axis runs over, the one named last changes fastest.
Arguments:
- forces: bfloat16 [2048, 768], P(('groups', 'row')), parts along dimension 0, may hold values from -6 to 6
- tiles: bfloat16 [32768, 96, 96], P(('groups', 'row')), parts along dimension 0, may hold values from -0.109375 to 0.109375
- tile_local: int32 [32768], P(('groups', 'row')), parts along dimension 0, may hold values from 0 to 63
- tile_slot: int32 [32768], P(('groups', 'row')), parts along dimension 0, may hold values from 0 to 255
- tile_flag: int32 [32768], P(('groups', 'row')), parts along dimension 0, may hold values 0 or 1
- want_list: int32 [32, 16, 16], P(('groups', 'row')), parts along dimension 0, may hold values from 0 to 63
Outputs:
- krylov_one: bfloat16 [2048, 768], P(('groups', 'row')), parts along dimension 0
- krylov_two: bfloat16 [2048, 768], P(('groups', 'row')), parts along dimension 0
There are 2 independent parts, one for each index of `groups`. A program takes and returns all parts, laid end to end along the dimension named above; each array names one. Nothing has to cross between parts.
All inputs are finite; a program needn't handle non-finite values. No bound on the sum of `tile_flag` on one device may be relied on, other than what follows from the above.
Results may differ from a plain program's by a relative error of at most 0.0041.
Values may be sent and summed in bfloat16 or wider, within the bound.
No kernel may reach another device: no remote copies, remote signals or barrier semaphores. Data moves between devices by JAX's collectives and lax.ppermute only.
A program may use at most 128 MiB of HBM per device.

v0:
```python
import jax
import jax.numpy as jnp
from jax import lax
from jax.sharding import PartitionSpec as P

NRHS = 8


def one_hot_table(index, count, kind):
    return (index[:, None] == jnp.arange(count, dtype=jnp.int32)[None, :]).astype(kind)


def pick_rows(table, values):
    return jnp.dot(table, values, preferred_element_type=jnp.float32).astype(jnp.bfloat16)


def sum_rows(table, partial_rows):
    return lax.dot_general(
        table,
        partial_rows,
        (((0,), (0,)), ((), ())),
        precision=lax.Precision.HIGHEST,
        preferred_element_type=jnp.float32,
    )


def per_device(forces, tiles, tile_local, tile_slot, tile_flag, want_list):
    peer_count = lax.axis_size("row")
    fibres = forces.shape[0]
    row_width = forces.shape[1]
    unknowns = tiles.shape[1]
    capacity = want_list.shape[2]
    blocks = tiles.shape[0]
    slot_total = peer_count * capacity
    wanted = want_list[0]
    mirror_gate = tile_flag.astype(jnp.float32)[:, None, None]
    local_pick = one_hot_table(tile_local, fibres, jnp.bfloat16)
    local_sum = one_hot_table(tile_local, fibres, jnp.float32)
    slot_pick = one_hot_table(tile_slot, slot_total, jnp.bfloat16)
    slot_sum = one_hot_table(tile_slot, slot_total, jnp.float32)
    global_rows = (jnp.arange(peer_count, dtype=jnp.int32)[:, None] * fibres + wanted).reshape(-1)
    global_pick = one_hot_table(global_rows, fibres * peer_count, jnp.bfloat16)
    global_sum = one_hot_table(global_rows, fibres * peer_count, jnp.float32)

    def operate(current):
        own_forces = pick_rows(local_pick, current).reshape(blocks, NRHS, unknowns)
        mirror = (
            jnp.einsum("kij,kri->krj", tiles, own_forces, preferred_element_type=jnp.float32)
            * mirror_gate
        )
        slot_part = sum_rows(slot_sum, mirror.reshape(blocks, row_width))
        all_rows = lax.all_gather(current, "row", axis=0, tiled=True)
        slot_forces = pick_rows(global_pick, all_rows)
        far_forces = pick_rows(slot_pick, slot_forces).reshape(blocks, NRHS, unknowns)
        direct = jnp.einsum("kij,krj->kri", tiles, far_forces, preferred_element_type=jnp.float32)
        own_part = sum_rows(local_sum, direct.reshape(blocks, row_width))
        dense_part = sum_rows(global_sum, slot_part)
        returned = lax.psum_scatter(dense_part, "row", scatter_dimension=0, tiled=True)
        return (own_part + returned).astype(jnp.bfloat16)

    krylov_one = operate(forces)
    krylov_two = operate(krylov_one)
    return (krylov_one, krylov_two)


def solution(mesh):
    in_specs = (
        P(("groups", "row"), None),
        P(("groups", "row"), None, None),
        P(("groups", "row")),
        P(("groups", "row")),
        P(("groups", "row")),
        P(("groups", "row"), None, None),
    )
    out_specs = (P(("groups", "row"), None), P(("groups", "row"), None))
    return jax.shard_map(
        per_device, mesh=mesh, in_specs=in_specs, out_specs=out_specs, check_vma=False
    )
```

profile of v0, /device:TPU:0, one launch (start us, length us, event | category | flops | bytes accessed | tf_op | source)
XLA Modules:
  0.0 256.3 jit_solution(7490937594834433806)
XLA Ops:
  8.0 29.6 %copy.17 = bf16[1024,96,96]{2,1,0:T(8,128)(2,1)} copy(bf16[1024,96,96]{0,2,1:T(8,128)(2,1)} %param.7) | data formatting | bytes 37748736 | tf_op args[1]
  39.5 3.3 %copy.19 = bf16[1024,8,96]{2,1,0:T(8,128)(2,1)S(1)} copy(bf16[1024,8,96]{0,2,1:T(8,128)(2,1)} %bitcast.30) | data formatting | bytes 3145728 | tf_op jit(solution)/shard_map/reshape | solution.py:46
  42.8 13.6 %broadcast_multiply_fusion.1 = f32[1024,8,96]{2,1,0:T(8,128)} fusion(f32[1024]{0:T(1024)S(1)} %convert_element_type.36, bf16[1024,8,96]{2,1,0:T(8,128)(2,1)S(1)} %copy.19, bf16[1024,96,96]{2,1,0:T(8,128)(2,1)} %copy.17), kind=kOutput, calls=%fused_computation.1 | convolution fusion | flops 151781376 | bytes 23597056 | tf_op jit(solution)/shard_map/kij,kri->krj/dot_general | solution.py:48
  56.4 3.9 %copy.21 = f32[1024,8,96]{0,2,1:T(8,128)S(1)} copy(f32[1024,8,96]{2,1,0:T(8,128)} %broadcast_multiply_fusion.1) | data formatting | bytes 6291456 | tf_op jit(solution)/shard_map/mul | solution.py:48
  60.5 2.0 fusion.7
  62.6 3.4 %fusion.3 = f32[1024,768]{1,0:T(8,128)} fusion(f32[256,768]{1,0:T(8,128)S(1)} %fusion.7, s32[256]{0:T(256)S(1)} %add.26), kind=kOutput, calls=%fused_computation.14 | convolution fusion | flops 2416181248 | bytes 3933184 | tf_op jit(solution)/shard_map/dot_general | solution.py:18
  66.2 4.0 %convolution_convert_fusion.3 = bf16[1024,768]{0,1:T(8,128)(2,1)} fusion(bf16[1024,768]{1,0:T(8,128)(2,1)} %all-gather.3.cloned.1.call-done, s32[256]{0:T(256)S(1)} %add.26, s32[1024]{0:T(1024)S(1)} %copy-done.2), kind=kOutput, calls=%fused_computation.5 | convolution fusion | flops 806813696 | bytes 3150848 | tf_op jit(solution)/shard_map/dot_general | solution.py:14
  70.3 3.3 %copy.16 = bf16[1024,8,96]{2,1,0:T(8,128)(2,1)S(1)} copy(bf16[1024,8,96]{0,2,1:T(8,128)(2,1)} %bitcast.33) | data formatting | bytes 3145728 | tf_op jit(solution)/shard_map/reshape | solution.py:54
  73.5 18.1 %fusion.26 = f32[1024,8,96]{2,1,0:T(8,128)} fusion(bf16[1024,8,96]{2,1,0:T(8,128)(2,1)S(1)} %copy.16, bf16[1024,96,96]{2,1,0:T(8,128)(2,1)} %copy.17), kind=kOutput, calls=%fused_computation.34 | convolution fusion | flops 150994944 | bytes 23592960 | tf_op jit(solution)/shard_map/kij,krj->kri/dot_general | solution.py:55
  91.6 3.9 %copy.18 = f32[1024,8,96]{0,2,1:T(8,128)S(1)} copy(f32[1024,8,96]{2,1,0:T(8,128)} %fusion.26) | data formatting | bytes 6291456 | tf_op jit(solution)/shard_map/kij,krj->kri/dot_general | solution.py:55
  95.5 39.6 %reduce-scatter.3.cloned.1.call-done = f32[64,768]{1,0:T(8,128)} async-done(((f32[1024,768]{1,0:T(8,128)}), f32[64,768]{1,0:T(8,128)}) %reduce-scatter.3.cloned.1.call-update) | async-done | bytes 196624 | tf_op jit(solution)/shard_map/reduce_scatter | solution.py:58
  135.1 3.5 %fusion = bf16[64,768]{1,0:T(8,128)(2,1)} fusion(f32[64,768]{1,0:T(8,128)} %reduce-scatter.3.cloned.1.call-done, f32[1024,768]{0,1:T(8,128)S(1)} %bitcast.28, s32[1024]{0:T(1024)S(1)} %copy-done.1), kind=kOutput, calls=%fused_computation.10 | convolution fusion | flops 604209152 | bytes 3444736 | tf_op jit(solution)/shard_map/dot_general | solution.py:18
  138.9 2.8 %convolution_convert_fusion = bf16[1024,768]{0,1:T(8,128)(2,1)} fusion(bf16[64,768]{1,0:T(8,128)(2,1)} %fusion, s32[1024]{0:T(1024)S(1)} %copy-done.1), kind=kOutput, calls=%fused_computation.2 | convolution fusion | flops 101515264 | bytes 1675264 | tf_op jit(solution)/shard_map/dot_general | solution.py:14
  141.7 3.3 %copy.25 = bf16[1024,8,96]{2,1,0:T(8,128)(2,1)S(1)} copy(bf16[1024,8,96]{0,2,1:T(8,128)(2,1)} %bitcast.31) | data formatting | bytes 3145728 | tf_op jit(solution)/shard_map/reshape | solution.py:46
  145.0 13.6 %broadcast_multiply_fusion = f32[1024,8,96]{2,1,0:T(8,128)} fusion(f32[1024]{0:T(1024)S(1)} %convert_element_type.36, bf16[1024,8,96]{2,1,0:T(8,128)(2,1)S(1)} %copy.25, bf16[1024,96,96]{2,1,0:T(8,128)(2,1)} %copy.17), kind=kOutput, calls=%fused_computation | convolution fusion | flops 151781376 | bytes 23597056 | tf_op jit(solution)/shard_map/kij,kri->krj/dot_general | solution.py:48
  158.5 3.9 %copy.27 = f32[1024,8,96]{0,2,1:T(8,128)S(1)} copy(f32[1024,8,96]{2,1,0:T(8,128)} %broadcast_multiply_fusion) | data formatting | bytes 6291456 | tf_op jit(solution)/shard_map/mul | solution.py:48
  164.4 3.4 %fusion.2 = f32[1024,768]{1,0:T(8,128)} fusion(f32[256,768]{1,0:T(8,128)S(1)} %fusion.5, s32[256]{0:T(256)S(1)} %add.26), kind=kOutput, calls=%fused_computation.13 | convolution fusion | flops 2416181248 | bytes 3933184 | tf_op jit(solution)/shard_map/dot_general | solution.py:18
  167.8 9.6 %all-gather.5.cloned.1.call-done = bf16[1024,768]{1,0:T(8,128)(2,1)} async-done(((bf16[64,768]{1,0:T(8,128)(2,1)}), bf16[1024,768]{1,0:T(8,128)(2,1)}) %all-gather.5.cloned.1.call-update) | async-done | bytes 1572880 | tf_op jit(solution)/shard_map/all_gather | solution.py:52
  177.5 4.0 %convolution_convert_fusion.2 = bf16[1024,768]{0,1:T(8,128)(2,1)} fusion(bf16[1024,768]{1,0:T(8,128)(2,1)} %all-gather.5.cloned.1.call-done, s32[256]{0:T(256)S(1)} %add.26, s32[1024]{0:T(1024)S(1)} %copy-done.2), kind=kOutput, calls=%fused_computation.4 | convolution fusion | flops 806813696 | bytes 3150848 | tf_op jit(solution)/shard_map/dot_general | solution.py:14
  181.5 3.3 %copy.22 = bf16[1024,8,96]{2,1,0:T(8,128)(2,1)S(1)} copy(bf16[1024,8,96]{0,2,1:T(8,128)(2,1)} %bitcast.32) | data formatting | bytes 3145728 | tf_op jit(solution)/shard_map/reshape | solution.py:54
  184.8 18.1 %fusion.27 = f32[1024,8,96]{2,1,0:T(8,128)} fusion(bf16[1024,8,96]{2,1,0:T(8,128)(2,1)S(1)} %copy.22, bf16[1024,96,96]{2,1,0:T(8,128)(2,1)} %copy.17), kind=kOutput, calls=%fused_computation.35 | convolution fusion | flops 150994944 | bytes 23592960 | tf_op jit(solution)/shard_map/kij,krj->kri/dot_general | solution.py:55
  202.9 3.9 %copy.24 = f32[1024,8,96]{0,2,1:T(8,128)S(1)} copy(f32[1024,8,96]{2,1,0:T(8,128)} %fusion.27) | data formatting | bytes 6291456 | tf_op jit(solution)/shard_map/kij,krj->kri/dot_general | solution.py:55
  206.7 39.6 %reduce-scatter.5.cloned.1.call-done = f32[64,768]{1,0:T(8,128)} async-done(((f32[1024,768]{1,0:T(8,128)}), f32[64,768]{1,0:T(8,128)}) %reduce-scatter.5.cloned.1.call-update) | async-done | bytes 196624 | tf_op jit(solution)/shard_map/reduce_scatter | solution.py:58
  246.3 3.5 %fusion.1 = bf16[64,768]{1,0:T(8,128)(2,1)} fusion(f32[64,768]{1,0:T(8,128)} %reduce-scatter.5.cloned.1.call-done, f32[1024,768]{0,1:T(8,128)S(1)} %bitcast.29, s32[1024]{0:T(1024)S(1)} %copy-done.1), kind=kOutput, calls=%fused_computation.11 | convolution fusion | flops 604209152 | bytes 3444736 | tf_op jit(solution)/shard_map/dot_general | solution.py:18
  (27 shorter events, 5.5 us)
Async XLA Ops:
  7.2 59.0 %all-gather.3.cloned.1.call-start = ((), (), s32[]{:S(2)}) async-start(), calls=%async_computation.2 | async-start | bytes 1671168 | tf_op jit(solution)/shard_map/all_gather | solution.py:52
  7.9 29.7 %copy-start.4 = (s32[1024]{0:T(1024)S(1)}, s32[1024]{0:T(1024)}, u32[]{:S(2)}) copy-start(s32[1024]{0:T(1024)} %param.10) | copy-start | bytes 12292
  7.9 29.7 %copy-start = (bf16[64,768]{1,0:T(8,128)(2,1)S(1)}, bf16[64,768]{1,0:T(8,128)(2,1)}, u32[]{:S(2)}) copy-start(bf16[64,768]{1,0:T(8,128)(2,1)} %param.6) | copy-start | bytes 294916
  7.9 29.7 %copy-start.1 = (s32[1024]{0:T(1024)S(1)}, s32[1024]{0:T(1024)}, u32[]{:S(2)}) copy-start(s32[1024]{0:T(1024)} %param.8) | copy-start | bytes 12292
  7.9 127.2 %reduce-scatter.3.cloned.1.call-start = ((), (), s32[]{:S(2)}) async-start(), calls=%async_computation.3 | async-start | bytes 3342336 | tf_op jit(solution)/shard_map/reduce_scatter | solution.py:58
  56.4 4.1 %copy-start.3 = (s32[1,16,16]{2,1,0:T(8,128)S(1)}, s32[1,16,16]{2,1,0:T(8,128)}, u32[]{:S(2)}) copy-start(s32[1,16,16]{2,1,0:T(8,128)} %param.11) | copy-start | bytes 3076
  56.4 4.1 %copy-start.2 = (s32[1024]{0:T(1024)S(1)}, s32[1024]{0:T(1024)}, u32[]{:S(2)}) copy-start(s32[1024]{0:T(1024)} %param.9) | copy-start | bytes 12292
  66.0 111.5 %all-gather.5.cloned.1.call-start = ((), (), s32[]{:S(2)}) async-start(), calls=%async_computation.4 | async-start | bytes 1671168 | tf_op jit(solution)/shard_map/all_gather | solution.py:52
  138.7 107.6 %reduce-scatter.5.cloned.1.call-start = ((), (), s32[]{:S(2)}) async-start(), calls=%async_computation.5 | async-start | bytes 3342336 | tf_op jit(solution)/shard_map/reduce_scatter | solution.py:58
Sparse Core Ops, SparseCore 0:
  10.3 42.3 all-gather.2
  66.1 69.0 reduce-scatter.2
  138.8 38.6 all-gather.4
  181.1 65.1 reduce-scatter.4
where the time goes:
time: 258 us; the launch traced here: 256 us
  matrix products  93.9 us (36%)
  waiting for transfers between devices  89.6 us (35%)
  local copies, waits for them, and re-layouts  58.4 us (23%)
  between operations  13.9 us (5%)
    reduce_scatter x2, waiting for transfers between devices, operate(): lax.psum_scatter(dense_part, 'row', scatter_dimension=0, tiled=True)  79.2 us
    dot_general x2, matrix products, operate(): jnp.einsum('kij,krj->kri', tiles, far_forces, preferred_element_type=jnp....  36.2 us
    unnamed x11, local copies, waits for them, and re-layouts  29.6 us
    dot_general x2, matrix products, operate(): jnp.einsum('kij,kri->krj', tiles, own_forces, preferred_element_type=jnp....  27.1 us
    dot_general x6, matrix products, sum_rows(): lax.dot_general(table, partial_rows, (((0,), (0,)), ((), ())), precision=...  17.8 us
    dot_general x4, matrix products, pick_rows(): jnp.dot(table, values, preferred_element_type=jnp.float32)  12.8 us
    all_gather x2, waiting for transfers between devices, operate(): all_rows = lax.all_gather(current, 'row', axis=0, tiled=True)  9.66 us
    mul x2, local copies, waits for them, and re-layouts, operate(): jnp.einsum('kij,kri->krj', tiles, own_forces, preferred_element_type=jnp....  7.74 us
  transfers between devices with their start and end apart: 4, of which 3 were waited for; matrix products, arithmetic and copies ran while one was open for 57% of the time, Pallas kernels for 0%

commit v1 on v0

--- a/solution.py
+++ b/solution.py
@@ -49,7 +49,14 @@
             * mirror_gate
         )
         slot_part = sum_rows(slot_sum, mirror.reshape(blocks, row_width))
-        all_rows = lax.all_gather(current, "row", axis=0, tiled=True)
+        size = lax.axis_size("row")
+        forward = [(i, (i + 1) % size) for i in range(size)]
+        parts = [current]
+        for hop in range(1, size):
+            parts = [lax.ppermute(parts[0], "row", forward), *parts]
+        result = jnp.concatenate(parts, axis=0)
+        places = (lax.axis_index("row") + 1) * parts[-1].shape[0]
+        all_rows = jnp.roll(result, places, axis=0)
         slot_forces = pick_rows(global_pick, all_rows)
         far_forces = pick_rows(slot_pick, slot_forces).reshape(blocks, NRHS, unknowns)
         direct = jnp.einsum("kij,krj->kri", tiles, far_forces, preferred_element_type=jnp.float32)

time: 258 us -> 356 us (1.38)
  waiting for transfers between devices: 89.6 us -> 177 us
  local copies, waits for them, and re-layouts: 58.4 us -> 67.4 us
    ppermute x0 -> x30, waiting for transfers between devices: none -> 165 us  [operate(): parts = [lax.ppermute(parts[0], 'row', forward), *parts]]
    reduce_scatter x2, waiting for transfers between devices: 79.2 us -> 12.7 us  [operate(): lax.psum_scatter(dense_part, 'row', scatter_dimension=0, tiled=True)]
    all_gather x2 -> x0, waiting for transfers between devices: 9.66 us -> none  [operate(): all_rows = lax.all_gather(current, 'row', axis=0, tiled=True)]
    unnamed x11 -> x65, local copies, waits for them, and re-layouts: 29.6 us -> 37.8 us
  transfers between devices with their start and end apart: 4 -> 32, of which waited for: 3 -> 29; matrix products, arithmetic and copies ran while one was open for 57% -> 43% of each run, Pallas kernels for 0% -> 0%
where the time goes in v1:
time: 356 us; the launch traced here: 354 us
  waiting for transfers between devices  177 us (50%)
  matrix products  93.6 us (26%)
  local copies, waits for them, and re-layouts  67.4 us (19%)
  between operations  14.5 us (4%)
    ppermute x30, waiting for transfers between devices, operate(): parts = [lax.ppermute(parts[0], 'row', forward), *parts]  165 us
    unnamed x65, local copies, waits for them, and re-layouts  37.8 us
    dot_general x2, matrix products, operate(): jnp.einsum('kij,krj->kri', tiles, far_forces, preferred_element_type=jnp....  35.9 us
    dot_general x2, matrix products, operate(): jnp.einsum('kij,kri->krj', tiles, own_forces, preferred_element_type=jnp....  27.1 us
    dot_general x6, matrix products, sum_rows(): lax.dot_general(table, partial_rows, (((0,), (0,)), ((), ())), precision=...  19.1 us
    reduce_scatter x2, waiting for transfers between devices, operate(): lax.psum_scatter(dense_part, 'row', scatter_dimension=0, tiled=True)  12.7 us
    dot_general x4, matrix products, pick_rows(): jnp.dot(table, values, preferred_element_type=jnp.float32)  11.5 us
    dot_general x2, local copies, waits for them, and re-layouts, operate(): jnp.einsum('kij,krj->kri', tiles, far_forces, preferred_element_type=jnp....  7.75 us
  transfers between devices with their start and end apart: 32, of which 29 were waited for; matrix products, arithmetic and copies ran while one was open for 43% of the time, Pallas kernels for 0%

profile of v1, /device:TPU:0, one launch (start us, length us, event | category | flops | bytes accessed | tf_op | source)
XLA Modules:
  0.0 354.1 jit_solution(13769869505717012495)
XLA Ops:
  7.7 7.5 %collective-permute-done = bf16[64,768]{1,0:T(8,128)(2,1)S(1)} collective-permute-done((bf16[64,768]{1,0:T(8,128)(2,1)}, bf16[64,768]{1,0:T(8,128)(2,1)S(1)}, u32[]{:S(2)}, u32[]{:S(2)}) %collective-permute-start) | collective-permute-done | bytes 98336 | tf_op jit(solution)/shard_map/ppermute | solution.py:56
  15.2 6.7 %collective-permute-done.1 = bf16[64,768]{1,0:T(8,128)(2,1)S(1)} collective-permute-done((bf16[64,768]{1,0:T(8,128)(2,1)S(1)}, bf16[64,768]{1,0:T(8,128)(2,1)S(1)}, u32[]{:S(2)}, u32[]{:S(2)}) %collective-permute-start.1) | collective-permute-done | bytes 98336 | tf_op jit(solution)/shard_map/ppermute | solution.py:56
  22.0 6.7 %collective-permute-done.2 = bf16[64,768]{1,0:T(8,128)(2,1)S(1)} collective-permute-done((bf16[64,768]{1,0:T(8,128)(2,1)S(1)}, bf16[64,768]{1,0:T(8,128)(2,1)S(1)}, u32[]{:S(2)}, u32[]{:S(2)}) %collective-permute-start.2) | collective-permute-done | bytes 98336 | tf_op jit(solution)/shard_map/ppermute | solution.py:56
  28.7 6.7 %collective-permute-done.3 = bf16[64,768]{1,0:T(8,128)(2,1)S(1)} collective-permute-done((bf16[64,768]{1,0:T(8,128)(2,1)S(1)}, bf16[64,768]{1,0:T(8,128)(2,1)S(1)}, u32[]{:S(2)}, u32[]{:S(2)}) %collective-permute-start.3) | collective-permute-done | bytes 98336 | tf_op jit(solution)/shard_map/ppermute | solution.py:56
  35.5 6.7 %collective-permute-done.4 = bf16[64,768]{1,0:T(8,128)(2,1)S(1)} collective-permute-done((bf16[64,768]{1,0:T(8,128)(2,1)S(1)}, bf16[64,768]{1,0:T(8,128)(2,1)S(1)}, u32[]{:S(2)}, u32[]{:S(2)}) %collective-permute-start.4) | collective-permute-done | bytes 98336 | tf_op jit(solution)/shard_map/ppermute | solution.py:56
  42.8 6.7 %collective-permute-done.5 = bf16[64,768]{1,0:T(8,128)(2,1)S(1)} collective-permute-done((bf16[64,768]{1,0:T(8,128)(2,1)S(1)}, bf16[64,768]{1,0:T(8,128)(2,1)S(1)}, u32[]{:S(2)}, u32[]{:S(2)}) %collective-permute-start.5) | collective-permute-done | bytes 98336 | tf_op jit(solution)/shard_map/ppermute | solution.py:56
  55.7 29.6 %copy.17 = bf16[1024,96,96]{2,1,0:T(8,128)(2,1)} copy(bf16[1024,96,96]{0,2,1:T(8,128)(2,1)} %param.9) | data formatting | bytes 37748736 | tf_op args[1]
  85.3 13.5 %broadcast_multiply_fusion.1 = f32[1024,8,96]{2,1,0:T(8,128)} fusion(f32[1024]{0:T(1024)S(1)} %convert_element_type.36, bf16[1024,8,96]{2,1,0:T(8,128)(2,1)S(1)} %copy.19, bf16[1024,96,96]{2,1,0:T(8,128)(2,1)} %copy.17), kind=kOutput, calls=%fused_computation.5 | convolution fusion | flops 151781376 | bytes 23597056 | tf_op jit(solution)/shard_map/kij,kri->krj/dot_general | solution.py:48
  123.5 6.7 %collective-permute-done.11 = bf16[64,768]{1,0:T(8,128)(2,1)S(1)} collective-permute-done((bf16[64,768]{1,0:T(8,128)(2,1)S(1)}, bf16[64,768]{1,0:T(8,128)(2,1)S(1)}, u32[]{:S(2)}, u32[]{:S(2)}) %collective-permute-start.11) | collective-permute-done | bytes 98336 | tf_op jit(solution)/shard_map/ppermute | solution.py:56
  130.3 6.7 %collective-permute-done.12 = bf16[64,768]{1,0:T(8,128)(2,1)S(1)} collective-permute-done((bf16[64,768]{1,0:T(8,128)(2,1)S(1)}, bf16[64,768]{1,0:T(8,128)(2,1)S(1)}, u32[]{:S(2)}, u32[]{:S(2)}) %collective-permute-start.12) | collective-permute-done | bytes 98336 | tf_op jit(solution)/shard_map/ppermute | solution.py:56
  137.0 6.7 %collective-permute-done.13 = bf16[64,768]{1,0:T(8,128)(2,1)S(1)} collective-permute-done((bf16[64,768]{1,0:T(8,128)(2,1)S(1)}, bf16[64,768]{1,0:T(8,128)(2,1)S(1)}, u32[]{:S(2)}, u32[]{:S(2)}) %collective-permute-start.13) | collective-permute-done | bytes 98336 | tf_op jit(solution)/shard_map/ppermute | solution.py:56
  143.8 6.7 %collective-permute-done.14 = bf16[64,768]{1,0:T(8,128)(2,1)S(1)} collective-permute-done((bf16[64,768]{1,0:T(8,128)(2,1)S(1)}, bf16[64,768]{1,0:T(8,128)(2,1)S(1)}, u32[]{:S(2)}, u32[]{:S(2)}) %collective-permute-start.14) | collective-permute-done | bytes 98336 | tf_op jit(solution)/shard_map/ppermute | solution.py:56
  160.2 17.9 %fusion.50 = f32[1024,8,96]{2,1,0:T(8,128)} fusion(bf16[1024,8,96]{2,1,0:T(8,128)(2,1)S(1)} %copy.16, bf16[1024,96,96]{2,1,0:T(8,128)(2,1)} %copy.17), kind=kOutput, calls=%fused_computation.78 | convolution fusion | flops 150994944 | bytes 23592960 | tf_op jit(solution)/shard_map/kij,krj->kri/dot_general | solution.py:62
  182.0 7.3 %reduce-scatter.3.cloned.1.call-done = f32[64,768]{1,0:T(8,128)} async-done(((f32[1024,768]{1,0:T(8,128)}), f32[64,768]{1,0:T(8,128)}) %reduce-scatter.3.cloned.1.call-update) | async-done | bytes 196624 | tf_op jit(solution)/shard_map/reduce_scatter | solution.py:65
  198.9 6.7 %collective-permute-done.16 = bf16[64,768]{1,0:T(8,128)(2,1)S(1)} collective-permute-done((bf16[64,768]{1,0:T(8,128)(2,1)S(1)}, bf16[64,768]{1,0:T(8,128)(2,1)S(1)}, u32[]{:S(2)}, u32[]{:S(2)}) %collective-permute-start.16) | collective-permute-done | bytes 98336 | tf_op jit(solution)/shard_map/ppermute | solution.py:56
  205.7 6.7 %collective-permute-done.17 = bf16[64,768]{1,0:T(8,128)(2,1)S(1)} collective-permute-done((bf16[64,768]{1,0:T(8,128)(2,1)S(1)}, bf16[64,768]{1,0:T(8,128)(2,1)S(1)}, u32[]{:S(2)}, u32[]{:S(2)}) %collective-permute-start.17) | collective-permute-done | bytes 98336 | tf_op jit(solution)/shard_map/ppermute | solution.py:56
  212.4 6.7 %collective-permute-done.18 = bf16[64,768]{1,0:T(8,128)(2,1)S(1)} collective-permute-done((bf16[64,768]{1,0:T(8,128)(2,1)S(1)}, bf16[64,768]{1,0:T(8,128)(2,1)S(1)}, u32[]{:S(2)}, u32[]{:S(2)}) %collective-permute-start.18) | collective-permute-done | bytes 98336 | tf_op jit(solution)/shard_map/ppermute | solution.py:56
  219.8 6.7 %collective-permute-done.19 = bf16[64,768]{1,0:T(8,128)(2,1)S(1)} collective-permute-done((bf16[64,768]{1,0:T(8,128)(2,1)S(1)}, bf16[64,768]{1,0:T(8,128)(2,1)S(1)}, u32[]{:S(2)}, u32[]{:S(2)}) %collective-permute-start.19) | collective-permute-done | bytes 98336 | tf_op jit(solution)/shard_map/ppermute | solution.py:56
  227.2 6.7 %collective-permute-done.20 = bf16[64,768]{1,0:T(8,128)(2,1)S(1)} collective-permute-done((bf16[64,768]{1,0:T(8,128)(2,1)S(1)}, bf16[64,768]{1,0:T(8,128)(2,1)S(1)}, u32[]{:S(2)}, u32[]{:S(2)}) %collective-permute-start.20) | collective-permute-done | bytes 98336 | tf_op jit(solution)/shard_map/ppermute | solution.py:56
  234.5 6.7 %collective-permute-done.21 = bf16[64,768]{1,0:T(8,128)(2,1)S(1)} collective-permute-done((bf16[64,768]{1,0:T(8,128)(2,1)S(1)}, bf16[64,768]{1,0:T(8,128)(2,1)S(1)}, u32[]{:S(2)}, u32[]{:S(2)}) %collective-permute-start.21) | collective-permute-done | bytes 98336 | tf_op jit(solution)/shard_map/ppermute | solution.py:56
  248.1 13.5 %broadcast_multiply_fusion = f32[1024,8,96]{2,1,0:T(8,128)} fusion(f32[1024]{0:T(1024)S(1)} %convert_element_type.36, bf16[1024,8,96]{2,1,0:T(8,128)(2,1)S(1)} %copy.25, bf16[1024,96,96]{2,1,0:T(8,128)(2,1)} %copy.17), kind=kOutput, calls=%fused_computation.4 | convolution fusion | flops 151781376 | bytes 23597056 | tf_op jit(solution)/shard_map/kij,kri->krj/dot_general | solution.py:48
  279.8 6.7 %collective-permute-done.26 = bf16[64,768]{1,0:T(8,128)(2,1)S(1)} collective-permute-done((bf16[64,768]{1,0:T(8,128)(2,1)S(1)}, bf16[64,768]{1,0:T(8,128)(2,1)S(1)}, u32[]{:S(2)}, u32[]{:S(2)}) %collective-permute-start.26) | collective-permute-done | bytes 98336 | tf_op jit(solution)/shard_map/ppermute | solution.py:56
  300.0 6.7 %collective-permute-done.29 = bf16[64,768]{1,0:T(8,128)(2,1)S(1)} collective-permute-done((bf16[64,768]{1,0:T(8,128)(2,1)S(1)}, bf16[64,768]{1,0:T(8,128)(2,1)S(1)}, u32[]{:S(2)}, u32[]{:S(2)}) %collective-permute-start.29) | collective-permute-done | bytes 98336 | tf_op jit(solution)/shard_map/ppermute | solution.py:56
  316.4 18.0 %fusion.51 = f32[1024,8,96]{2,1,0:T(8,128)} fusion(bf16[1024,8,96]{2,1,0:T(8,128)(2,1)S(1)} %copy.22, bf16[1024,96,96]{2,1,0:T(8,128)(2,1)} %copy.17), kind=kOutput, calls=%fused_computation.79 | convolution fusion | flops 150994944 | bytes 23592960 | tf_op jit(solution)/shard_map/kij,krj->kri/dot_general | solution.py:62
  (137 shorter events, 117.6 us)
Async XLA Ops:
  7.2 182.1 %reduce-scatter.3.cloned.1.call-start = ((), (), s32[]{:S(2)}) async-start(), calls=%async_computation.2 | async-start | bytes 3342336 | tf_op jit(solution)/shard_map/reduce_scatter | solution.py:65
  7.2 8.0 %collective-permute-start = (bf16[64,768]{1,0:T(8,128)(2,1)}, bf16[64,768]{1,0:T(8,128)(2,1)S(1)}, u32[]{:S(2)}, u32[]{:S(2)}) collective-permute-start(bf16[64,768]{1,0:T(8,128)(2,1)} %param.8), channel_id=1, source_target_pairs={{0,1},{1,2},{2,3},{3,4},{4,5},{5,6},{6,7},{7,8},{8,9},{9,10},{10,1... | collective-permute-start | bytes 294920 | tf_op jit(solution)/shard_map/ppermute | solution.py:56
  15.2 6.7 %collective-permute-start.1 = (bf16[64,768]{1,0:T(8,128)(2,1)S(1)}, bf16[64,768]{1,0:T(8,128)(2,1)S(1)}, u32[]{:S(2)}, u32[]{:S(2)}) collective-permute-start(bf16[64,768]{1,0:T(8,128)(2,1)S(1)} %collective-permute-done), channel_id=1, source_target_pairs={{0,1},{1,2},{2,3},{3,4},{4,5},{5,6},{6,7},{7,8},{8,9},{9,10},{10,1... | collective-permute-start | bytes 294920 | tf_op jit(solution)/shard_map/ppermute | solution.py:56
  22.0 6.7 %collective-permute-start.2 = (bf16[64,768]{1,0:T(8,128)(2,1)S(1)}, bf16[64,768]{1,0:T(8,128)(2,1)S(1)}, u32[]{:S(2)}, u32[]{:S(2)}) collective-permute-start(bf16[64,768]{1,0:T(8,128)(2,1)S(1)} %collective-permute-done.1), channel_id=1, source_target_pairs={{0,1},{1,2},{2,3},{3,4},{4,5},{5,6},{6,7},{7,8},{8,9},{9,10},{10,1... | collective-permute-start | bytes 294920 | tf_op jit(solution)/shard_map/ppermute | solution.py:56
  28.7 6.7 %collective-permute-start.3 = (bf16[64,768]{1,0:T(8,128)(2,1)S(1)}, bf16[64,768]{1,0:T(8,128)(2,1)S(1)}, u32[]{:S(2)}, u32[]{:S(2)}) collective-permute-start(bf16[64,768]{1,0:T(8,128)(2,1)S(1)} %collective-permute-done.2), channel_id=1, source_target_pairs={{0,1},{1,2},{2,3},{3,4},{4,5},{5,6},{6,7},{7,8},{8,9},{9,10},{10,1... | collective-permute-start | bytes 294920 | tf_op jit(solution)/shard_map/ppermute | solution.py:56
  35.4 6.7 %collective-permute-start.4 = (bf16[64,768]{1,0:T(8,128)(2,1)S(1)}, bf16[64,768]{1,0:T(8,128)(2,1)S(1)}, u32[]{:S(2)}, u32[]{:S(2)}) collective-permute-start(bf16[64,768]{1,0:T(8,128)(2,1)S(1)} %collective-permute-done.3), channel_id=1, source_target_pairs={{0,1},{1,2},{2,3},{3,4},{4,5},{5,6},{6,7},{7,8},{8,9},{9,10},{10,1... | collective-permute-start | bytes 294920 | tf_op jit(solution)/shard_map/ppermute | solution.py:56
  49.6 35.7 %collective-permute-start.6 = (bf16[64,768]{1,0:T(8,128)(2,1)S(1)}, bf16[64,768]{1,0:T(8,128)(2,1)}, u32[]{:S(2)}, u32[]{:S(2)}) collective-permute-start(bf16[64,768]{1,0:T(8,128)(2,1)S(1)} %collective-permute-done.5), channel_id=1, source_target_pairs={{0,1},{1,2},{2,3},{3,4},{4,5},{5,6},{6,7},{7,8},{8,9},{9,10},{10,1... | collective-permute-start | bytes 294920 | tf_op jit(solution)/shard_map/ppermute | solution.py:56
  85.3 17.4 %collective-permute-start.7 = (bf16[64,768]{1,0:T(8,128)(2,1)}, bf16[64,768]{1,0:T(8,128)(2,1)}, u32[]{:S(2)}, u32[]{:S(2)}) collective-permute-start(bf16[64,768]{1,0:T(8,128)(2,1)} %collective-permute-done.6), channel_id=1, source_target_pairs={{0,1},{1,2},{2,3},{3,4},{4,5},{5,6},{6,7},{7,8},{8,9},{9,10},{10,1... | collective-permute-start | bytes 294920 | tf_op jit(solution)/shard_map/ppermute | solution.py:56
  102.7 7.1 %collective-permute-start.8 = (bf16[64,768]{1,0:T(8,128)(2,1)}, bf16[64,768]{1,0:T(8,128)(2,1)}, u32[]{:S(2)}, u32[]{:S(2)}) collective-permute-start(bf16[64,768]{1,0:T(8,128)(2,1)} %collective-permute-done.7), channel_id=1, source_target_pairs={{0,1},{1,2},{2,3},{3,4},{4,5},{5,6},{6,7},{7,8},{8,9},{9,10},{10,1... | collective-permute-start | bytes 294920 | tf_op jit(solution)/shard_map/ppermute | solution.py:56
  109.8 6.9 %collective-permute-start.9 = (bf16[64,768]{1,0:T(8,128)(2,1)}, bf16[64,768]{1,0:T(8,128)(2,1)S(1)}, u32[]{:S(2)}, u32[]{:S(2)}) collective-permute-start(bf16[64,768]{1,0:T(8,128)(2,1)} %collective-permute-done.8), channel_id=1, source_target_pairs={{0,1},{1,2},{2,3},{3,4},{4,5},{5,6},{6,7},{7,8},{8,9},{9,10},{10,1... | collective-permute-start | bytes 294920 | tf_op jit(solution)/shard_map/ppermute | solution.py:56
  121.3 222.4 %reduce-scatter.5.cloned.1.call-start = ((), (), s32[]{:S(2)}) async-start(), calls=%async_computation.3 | async-start | bytes 3342336 | tf_op jit(solution)/shard_map/reduce_scatter | solution.py:65
  130.3 6.7 %collective-permute-start.12 = (bf16[64,768]{1,0:T(8,128)(2,1)S(1)}, bf16[64,768]{1,0:T(8,128)(2,1)S(1)}, u32[]{:S(2)}, u32[]{:S(2)}) collective-permute-start(bf16[64,768]{1,0:T(8,128)(2,1)S(1)} %collective-permute-done.11), channel_id=1, source_target_pairs={{0,1},{1,2},{2,3},{3,4},{4,5},{5,6},{6,7},{7,8},{8,9},{9,10},{10,1... | collective-permute-start | bytes 294920 | tf_op jit(solution)/shard_map/ppermute | solution.py:56
  143.7 6.7 %collective-permute-start.14 = (bf16[64,768]{1,0:T(8,128)(2,1)S(1)}, bf16[64,768]{1,0:T(8,128)(2,1)S(1)}, u32[]{:S(2)}, u32[]{:S(2)}) collective-permute-start(bf16[64,768]{1,0:T(8,128)(2,1)S(1)} %collective-permute-done.13), channel_id=1, source_target_pairs={{0,1},{1,2},{2,3},{3,4},{4,5},{5,6},{6,7},{7,8},{8,9},{9,10},{10,1... | collective-permute-start | bytes 294920 | tf_op jit(solution)/shard_map/ppermute | solution.py:56
  192.1 6.8 %collective-permute-start.15 = (bf16[64,768]{1,0:T(8,128)(2,1)S(1)}, bf16[64,768]{1,0:T(8,128)(2,1)S(1)}, u32[]{:S(2)}, u32[]{:S(2)}) collective-permute-start(bf16[64,768]{1,0:T(8,128)(2,1)S(1)} %fusion.16), channel_id=1, source_target_pairs={{0,1},{1,2},{2,3},{3,4},{4,5},{5,6},{6,7},{7,8},{8,9},{9,10},{10,1... | collective-permute-start | bytes 294920 | tf_op jit(solution)/shard_map/ppermute | solution.py:56
  205.7 6.7 %collective-permute-start.17 = (bf16[64,768]{1,0:T(8,128)(2,1)S(1)}, bf16[64,768]{1,0:T(8,128)(2,1)S(1)}, u32[]{:S(2)}, u32[]{:S(2)}) collective-permute-start(bf16[64,768]{1,0:T(8,128)(2,1)S(1)} %collective-permute-done.16), channel_id=1, source_target_pairs={{0,1},{1,2},{2,3},{3,4},{4,5},{5,6},{6,7},{7,8},{8,9},{9,10},{10,1... | collective-permute-start | bytes 294920 | tf_op jit(solution)/shard_map/ppermute | solution.py:56
  219.8 6.7 %collective-permute-start.19 = (bf16[64,768]{1,0:T(8,128)(2,1)S(1)}, bf16[64,768]{1,0:T(8,128)(2,1)S(1)}, u32[]{:S(2)}, u32[]{:S(2)}) collective-permute-start(bf16[64,768]{1,0:T(8,128)(2,1)S(1)} %collective-permute-done.18), channel_id=1, source_target_pairs={{0,1},{1,2},{2,3},{3,4},{4,5},{5,6},{6,7},{7,8},{8,9},{9,10},{10,1... | collective-permute-start | bytes 294920 | tf_op jit(solution)/shard_map/ppermute | solution.py:56
  227.2 6.7 %collective-permute-start.20 = (bf16[64,768]{1,0:T(8,128)(2,1)S(1)}, bf16[64,768]{1,0:T(8,128)(2,1)S(1)}, u32[]{:S(2)}, u32[]{:S(2)}) collective-permute-start(bf16[64,768]{1,0:T(8,128)(2,1)S(1)} %collective-permute-done.19), channel_id=1, source_target_pairs={{0,1},{1,2},{2,3},{3,4},{4,5},{5,6},{6,7},{7,8},{8,9},{9,10},{10,1... | collective-permute-start | bytes 294920 | tf_op jit(solution)/shard_map/ppermute | solution.py:56
  234.5 6.7 %collective-permute-start.21 = (bf16[64,768]{1,0:T(8,128)(2,1)S(1)}, bf16[64,768]{1,0:T(8,128)(2,1)S(1)}, u32[]{:S(2)}, u32[]{:S(2)}) collective-permute-start(bf16[64,768]{1,0:T(8,128)(2,1)S(1)} %collective-permute-done.20), channel_id=1, source_target_pairs={{0,1},{1,2},{2,3},{3,4},{4,5},{5,6},{6,7},{7,8},{8,9},{9,10},{10,1... | collective-permute-start | bytes 294920 | tf_op jit(solution)/shard_map/ppermute | solution.py:56
  241.3 6.8 %collective-permute-start.22 = (bf16[64,768]{1,0:T(8,128)(2,1)S(1)}, bf16[64,768]{1,0:T(8,128)(2,1)}, u32[]{:S(2)}, u32[]{:S(2)}) collective-permute-start(bf16[64,768]{1,0:T(8,128)(2,1)S(1)} %collective-permute-done.21), channel_id=1, source_target_pairs={{0,1},{1,2},{2,3},{3,4},{4,5},{5,6},{6,7},{7,8},{8,9},{9,10},{10,1... | collective-permute-start | bytes 294920 | tf_op jit(solution)/shard_map/ppermute | solution.py:56
  248.1 17.4 %collective-permute-start.23 = (bf16[64,768]{1,0:T(8,128)(2,1)}, bf16[64,768]{1,0:T(8,128)(2,1)}, u32[]{:S(2)}, u32[]{:S(2)}) collective-permute-start(bf16[64,768]{1,0:T(8,128)(2,1)} %collective-permute-done.22), channel_id=1, source_target_pairs={{0,1},{1,2},{2,3},{3,4},{4,5},{5,6},{6,7},{7,8},{8,9},{9,10},{10,1... | collective-permute-start | bytes 294920 | tf_op jit(solution)/shard_map/ppermute | solution.py:56
  265.5 7.3 %collective-permute-start.24 = (bf16[64,768]{1,0:T(8,128)(2,1)}, bf16[64,768]{1,0:T(8,128)(2,1)}, u32[]{:S(2)}, u32[]{:S(2)}) collective-permute-start(bf16[64,768]{1,0:T(8,128)(2,1)} %collective-permute-done.23), channel_id=1, source_target_pairs={{0,1},{1,2},{2,3},{3,4},{4,5},{5,6},{6,7},{7,8},{8,9},{9,10},{10,1... | collective-permute-start | bytes 294920 | tf_op jit(solution)/shard_map/ppermute | solution.py:56
  272.8 6.9 %collective-permute-start.25 = (bf16[64,768]{1,0:T(8,128)(2,1)}, bf16[64,768]{1,0:T(8,128)(2,1)S(1)}, u32[]{:S(2)}, u32[]{:S(2)}) collective-permute-start(bf16[64,768]{1,0:T(8,128)(2,1)} %collective-permute-done.24), channel_id=1, source_target_pairs={{0,1},{1,2},{2,3},{3,4},{4,5},{5,6},{6,7},{7,8},{8,9},{9,10},{10,1... | collective-permute-start | bytes 294920 | tf_op jit(solution)/shard_map/ppermute | solution.py:56
  279.8 6.7 %collective-permute-start.26 = (bf16[64,768]{1,0:T(8,128)(2,1)S(1)}, bf16[64,768]{1,0:T(8,128)(2,1)S(1)}, u32[]{:S(2)}, u32[]{:S(2)}) collective-permute-start(bf16[64,768]{1,0:T(8,128)(2,1)S(1)} %collective-permute-done.25), channel_id=1, source_target_pairs={{0,1},{1,2},{2,3},{3,4},{4,5},{5,6},{6,7},{7,8},{8,9},{9,10},{10,1... | collective-permute-start | bytes 294920 | tf_op jit(solution)/shard_map/ppermute | solution.py:56
  300.0 6.7 %collective-permute-start.29 = (bf16[64,768]{1,0:T(8,128)(2,1)S(1)}, bf16[64,768]{1,0:T(8,128)(2,1)S(1)}, u32[]{:S(2)}, u32[]{:S(2)}) collective-permute-start(bf16[64,768]{1,0:T(8,128)(2,1)S(1)} %collective-permute-done.28), channel_id=1, source_target_pairs={{0,1},{1,2},{2,3},{3,4},{4,5},{5,6},{6,7},{7,8},{8,9},{9,10},{10,1... | collective-permute-start | bytes 294920 | tf_op jit(solution)/shard_map/ppermute | solution.py:56
  (25 other events, 475.0 us)
Sparse Core Ops, SparseCore 0:
  121.4 67.8 reduce-scatter.2
  276.3 67.3 reduce-scatter.4
